TPU v7x, 32 devices: a whole 2x2x4 slice. The times are simulated.
32 devices in a mesh: seq: 8 (over z, x), batch: 4 (over y, core).
Axes of the slice: x: 2, y: 2, z: 4, core: 2. Of those that a mesh axis runs over, the one named last changes fastest.
Arguments:
- inputs: float32 [4, 1024, 768], P('batch', 'seq'), may hold values from -6 to 6
- norm_gain: float32 [768], replicated, may hold values from 0.5 to 1.5
- input_projection_weight: float32 [768, 3072], replicated, may hold values from -0.21875 to 0.21875
- conv_weight: float32 [4, 1536], replicated, may hold values from -3 to 3
- conv_bias: float32 [1536], replicated, may hold values from -3 to 3
- x_proj: float32 [1536, 80], replicated, may hold values from -0.15625 to 0.15625
- step_proj: float32 [48, 1536], replicated, may hold values from -0.875 to 0.875
- step_bias: float32 [1536], replicated, may hold values from -3 to -1
- decay_code: int32 [1536], replicated, may hold values from 0 to 9
- decay_log: float32 [1536, 16], replicated, may hold values from -5 to -1.5
- skip_gain: float32 [1536], replicated, may hold values from 0.5 to 1.5
- output_projection_weight: float32 [1536, 768], replicated, may hold values from -0.15625 to 0.15625
- cotangent: float32 [4, 1024, 768], P('batch', 'seq'), may hold values from -6 to 6
Outputs:
- block_out: float32 [4, 1024, 768], P('batch', 'seq')
- input_grad: float32 [4, 1024, 768], P('batch', 'seq')
- norm_gain_grad: float32 [768], replicated
- in_proj_grad: float32 [768, 3072], replicated
- conv_weight_grad: float32 [4, 1536], replicated
- conv_bias_grad: float32 [1536], replicated
- x_proj_grad: float32 [1536, 80], replicated
- step_proj_grad: float32 [48, 1536], replicated
- step_bias_grad: float32 [1536], replicated
- decay_log_grad: float32 [1536, 16], replicated
- skip_gain_grad: float32 [1536], replicated
- out_proj_grad: float32 [1536, 768], replicated
All inputs are finite; a program needn't handle non-finite values.
Results may differ from a plain program's by a relative error of at most 0.0003.
Values sent between devices are 32-bit elements; how exact they have to be, the bound alone decides.
A program may use at most 128 MiB of HBM per device.

v0:
```python
from functools import partial
import jax
import jax.numpy as jnp
from jax import lax
from jax.sharding import PartitionSpec as P

QB = 32
MATMUL_ACCURACY = lax.Precision.HIGHEST
EPSILON = 1e-05


def shifted(x, axis, by):
    length = lax.axis_size(axis)
    pairs = [(i, i + by) for i in range(length) if 0 <= i + by < length]
    return lax.ppermute(x, axis, pairs)


def prefix(value, axis, join, neutral, backward):
    count, mine = (lax.axis_size(axis), lax.axis_index(axis))
    pieces = jax.tree.map(lambda part: lax.all_gather(part, axis), value)
    if backward:
        pieces = jax.tree.map(lambda part: part[::-1], pieces)
        mine = count - 1 - mine
    subtotal = jax.tree.map(
        lambda part, zero: jnp.full_like(part, 0) + jnp.asarray(zero, part.dtype), value, neutral
    )

    def turn(position, subtotal):
        longer = join(subtotal, jax.tree.map(lambda part: part[position], pieces))
        return jax.tree.map(lambda new, old: jnp.where(position < mine, new, old), longer, subtotal)

    return lax.fori_loop(0, count - 1, turn, subtotal)


def matmul(left, right):
    return jnp.dot(left, right, precision=MATMUL_ACCURACY, preferred_element_type=jnp.float32)


def silu_grad(value):
    sigma = jax.nn.sigmoid(value)
    return sigma * (1.0 + value * (1.0 - sigma))


def pair_combine(first, second):
    return (first[0] * second[0], first[1] * second[0] + second[1])


def block_states(factor, source, start):
    cumulative_decay_factor, cum_source = lax.associative_scan(
        pair_combine, (factor, source), axis=0
    )
    return cum_source + cumulative_decay_factor * start[None]


def join_carry(negative_decay_rate, earlier, later):
    return (
        earlier[0] + later[0],
        earlier[1] * jnp.exp(negative_decay_rate[None] * later[0][:, None, :]) + later[1],
    )


def adjoint(factor, values, carry):
    alpha = jnp.concatenate([factor[1:], jnp.ones_like(factor[:1])], axis=0)
    return block_states(alpha[::-1], values[::-1], carry)[::-1]


def shards(
    inputs,
    norm_gain,
    input_projection_weight,
    conv_weight,
    conv_bias,
    x_proj,
    step_proj,
    step_bias,
    decay_code,
    decay_log,
    skip_gain,
    output_projection_weight,
    cotangent,
):
    seqs, group, width = inputs.shape
    inner = input_projection_weight.shape[1] // 2
    rank = step_proj.shape[0]
    states = decay_log.shape[1]
    taps = conv_weight.shape[0]
    blocks = group // QB
    rows = seqs * group

    def to_blocks(value):
        cols = value.shape[-1]
        return jnp.swapaxes(value.reshape(seqs, group, cols), 0, 1).reshape(blocks, QB, seqs, cols)

    def from_blocks(value):
        cols = value.shape[-1]
        return jnp.swapaxes(value.reshape(group, seqs, cols), 0, 1).reshape(rows, cols)

    def unpack(packed_blk):
        step_blk = packed_blk[..., :inner]
        mixed_blk = packed_blk[..., inner : 2 * inner]
        b_blk = packed_blk[..., 2 * inner : 2 * inner + states]
        c_blk = packed_blk[..., 2 * inner + states :]
        return (step_blk, mixed_blk, b_blk, c_blk)

    flat_in = inputs.reshape(rows, width)
    rms = lax.rsqrt(jnp.mean(flat_in * flat_in, axis=1, keepdims=True) + EPSILON)
    normalized_input = flat_in * rms * norm_gain
    mixer_and_gate = matmul(normalized_input, input_projection_weight)
    hidden_x = mixer_and_gate[:, :inner].reshape(seqs, group, inner)
    gate_z = mixer_and_gate[:, inner:]
    rim = shifted(hidden_x[:, group - taps + 1 :], "seq", 1)
    padded = jnp.concatenate([rim, hidden_x], axis=1)
    conv = conv_bias + conv_weight[0] * padded[:, 0:group]
    for k in range(1, taps):
        conv = conv + conv_weight[k] * padded[:, k : k + group]
    conv = conv.reshape(rows, inner)
    mixed = jax.nn.silu(conv)
    proj = matmul(mixed, x_proj)
    low_rank = proj[:, :rank]
    pre = matmul(low_rank, step_proj) + step_bias - 0.5 * decay_code.astype(jnp.float32)
    step = jax.nn.softplus(pre)
    negative_decay_rate = -jnp.exp(decay_log).T
    packed_blocks = to_blocks(jnp.concatenate([step, mixed, proj[:, rank:]], axis=1))
    zero_state = jnp.zeros((seqs, states, inner), jnp.float32)
    zero_sum = jnp.zeros((seqs, inner), jnp.float32)

    def terms(step_blk, mixed_blk, b_blk):
        factor = jnp.exp(step_blk[:, :, None, :] * negative_decay_rate)
        source = (step_blk * mixed_blk)[:, :, None, :] * b_blk[:, :, :, None]
        return (factor, source)

    def local_block(state, packed_blk):
        step_blk, mixed_blk, b_blk, c_blk = unpack(packed_blk)
        factor, source = terms(step_blk, mixed_blk, b_blk)
        held = block_states(factor, source, state)
        output = jnp.sum(held * c_blk[:, :, :, None], axis=2)
        return (held[-1], (output, state))

    end_state, (local_out, local_starts) = lax.scan(local_block, zero_state, packed_blocks)
    group_sum = jnp.sum(step.reshape(seqs, group, inner), axis=1)
    combine = partial(join_carry, negative_decay_rate)
    identity = (jnp.zeros_like(group_sum), zero_state)
    start_state = prefix((group_sum, end_state), "seq", combine, identity, False)[1]

    def shift_in(total, data):
        packed_blk, out_blk = data
        step_blk, mixed_blk, b_blk, c_blk = unpack(packed_blk)
        inside = total[None] + jnp.cumsum(step_blk, axis=0)
        decay = jnp.exp(inside[:, :, None, :] * negative_decay_rate)
        output = out_blk + jnp.sum(decay * start_state[None] * c_blk[:, :, :, None], axis=2)
        begin = jnp.exp(total[:, None, :] * negative_decay_rate) * start_state
        return (inside[-1], (output, begin))

    _, (scanned, begins) = lax.scan(shift_in, zero_sum, (packed_blocks, local_out))
    starts = local_starts + begins
    result = from_blocks(scanned) + skip_gain * mixed
    gate_act = jax.nn.silu(gate_z)
    gate_applied_output = result * gate_act
    block_out = (flat_in + matmul(gate_applied_output, output_projection_weight)).reshape(
        seqs, group, width
    )
    flat_cot = cotangent.reshape(rows, width)
    d_gated = matmul(flat_cot, output_projection_weight.T)
    out_grad = matmul(gate_applied_output.T, flat_cot)
    d_result = d_gated * gate_act
    d_gate = d_gated * result * silu_grad(gate_z)
    skip_grad = jnp.sum(d_result * mixed, axis=0)
    dres_blocks = to_blocks(d_result)

    def collect_back(acc, data):
        total, lam_in = acc
        packed_blk, dres_blk = data
        step_blk, mixed_blk, b_blk, c_blk = unpack(packed_blk)
        inside = total[None] + jnp.cumsum(step_blk, axis=0)
        decay = jnp.exp(inside[:, :, None, :] * negative_decay_rate)
        lam_in = lam_in + jnp.sum(decay * c_blk[:, :, :, None] * dres_blk[:, :, None, :], axis=0)
        return ((inside[-1], lam_in), None)

    (_, later_in), _ = lax.scan(collect_back, (zero_sum, zero_state), (packed_blocks, dres_blocks))
    after_state = prefix((group_sum, later_in), "seq", combine, identity, True)[1]

    def full_back(carry, data):
        lam_next, rate_acc = carry
        packed_blk, dres_blk, start = data
        step_blk, mixed_blk, b_blk, c_blk = unpack(packed_blk)
        factor, source = terms(step_blk, mixed_blk, b_blk)
        held = block_states(factor, source, start)
        prior = jnp.concatenate([start[None], held[:-1]], axis=0)
        lam = adjoint(factor, c_blk[:, :, :, None] * dres_blk[:, :, None, :], lam_next)
        c_grad = jnp.sum(held * dres_blk[:, :, None, :], axis=3)
        decayed = lam * prior * factor
        lam_b = jnp.sum(lam * b_blk[:, :, :, None], axis=2)
        step_grad = jnp.sum(decayed * negative_decay_rate, axis=2) + mixed_blk * lam_b
        rate_acc = rate_acc + jnp.sum(decayed * step_blk[:, :, None, :], axis=(0, 1))
        mixed_scan = step_blk * lam_b
        b_grad = jnp.sum(lam * (step_blk * mixed_blk)[:, :, None, :], axis=3)
        joined = jnp.concatenate([step_grad, mixed_scan, b_grad, c_grad], axis=-1)
        return ((factor[0] * lam[0], rate_acc), joined)

    rate_zero = jnp.zeros((states, inner), jnp.float32)
    (_, rate_sum), back_blocks = lax.scan(
        full_back, (after_state, rate_zero), (packed_blocks, dres_blocks, starts), reverse=True
    )
    back_rows = from_blocks(back_blocks)
    step_grad = back_rows[:, :inner]
    mixed_scan = back_rows[:, inner : 2 * inner]
    b_grad = back_rows[:, 2 * inner : 2 * inner + states]
    c_grad = back_rows[:, 2 * inner + states :]
    decay_grad = (rate_sum * negative_decay_rate).T
    pre_grad = step_grad * jax.nn.sigmoid(pre)
    bias_grad = jnp.sum(pre_grad, axis=0)
    step_proj_grad = matmul(low_rank.T, pre_grad)
    proj_grad = jnp.concatenate([matmul(pre_grad, step_proj.T), b_grad, c_grad], axis=1)
    x_proj_grad = matmul(mixed.T, proj_grad)
    mixed_grad = mixed_scan + d_result * skip_gain + matmul(proj_grad, x_proj.T)
    conv_grad = (mixed_grad * silu_grad(conv)).reshape(seqs, group, inner)
    tap_grads = jnp.stack(
        [jnp.sum(conv_grad * padded[:, k : k + group], axis=(0, 1)) for k in range(taps)]
    )
    conv_bias_grad = jnp.sum(conv_grad, axis=(0, 1))
    spread = jnp.zeros((seqs, group + taps - 1, inner), jnp.float32)
    for k in range(taps):
        spread = spread.at[:, k : k + group].add(conv_weight[k] * conv_grad)
    back_rim = shifted(spread[:, : taps - 1], "seq", -1)
    x_grad = spread[:, taps - 1 :].at[:, group - taps + 1 :].add(back_rim)
    both_grad = jnp.concatenate([x_grad.reshape(rows, inner), d_gate], axis=1)
    in_grad = matmul(normalized_input.T, both_grad)
    normed_grad = matmul(both_grad, input_projection_weight.T)
    gain_grad = jnp.sum(normed_grad * flat_in * rms, axis=0)
    weighted = normed_grad * norm_gain
    input_grad = (
        rms * weighted
        - rms * rms * rms * flat_in * jnp.mean(weighted * flat_in, axis=1, keepdims=True)
        + flat_cot
    )
    input_grad = input_grad.reshape(seqs, group, width)
    summed_all = lax.psum(
        (
            gain_grad,
            in_grad,
            tap_grads,
            conv_bias_grad,
            x_proj_grad,
            step_proj_grad,
            bias_grad,
            decay_grad,
            skip_grad,
            out_grad,
        ),
        ("seq", "batch"),
    )
    summed = summed_all[:8]
    skip_sum = summed_all[8]
    out_sum = summed_all[9]
    return (
        block_out,
        input_grad,
        summed[0],
        summed[1],
        summed[2],
        summed[3],
        summed[4],
        summed[5],
        summed[6],
        summed[7],
        skip_sum,
        out_sum,
    )


def solution(mesh):
    return jax.shard_map(
        shards,
        mesh=mesh,
        in_specs=(
            P("batch", "seq", None),
            P(),
            P(),
            P(),
            P(),
            P(),
            P(),
            P(),
            P(),
            P(),
            P(),
            P(),
            P("batch", "seq", None),
        ),
        out_specs=(
            P("batch", "seq", None),
            P("batch", "seq", None),
            P(),
            P(),
            P(),
            P(),
            P(),
            P(),
            P(),
            P(),
            P(),
            P(),
        ),
        check_vma=False,
    )
```

profile of v0, /device:TPU:0, one launch (start us, length us, event | category | flops | bytes accessed | tf_op | source)
XLA Modules:
  0.0 2101.1 jit_solution(8007326374587562995)
XLA Ops:
  37.9 33.2 %all-gather.3 = f32[8,1,1536]{2,1,0:T(1,128)S(1)} all-gather(f32[1,1,1536]{2,1,0:T(1,128)S(1)} %reshape.758), channel_id=2, replica_groups=mesh['seq'=8,'batch'=4] {'seq'}, dimensions={0}, use_global_device_ids=true | all-gather | bytes 55296 | tf_op jit(solution)/shard_map/all_gather | solution.py:20
  75.0 414.5 %while.93 = (s32[]{:T(128)}, f32[1,16,1536]{2,1,0:T(8,128)}, f32[4,32,1,1536]{3,2,1,0:T(1,128)}, f32[4,1,16,1536]{3,2,1,0:T(8,128)}, f32[4,32,1,3104]{3,2,1,0:T(...) while((s32[]{:T(128)}, f32[1,16,1536]{2,1,0:T(8,128)}, f32[4,32,1,1536]{3,2,1,0:T(1,128)}, ...), condition=%wide.region_3.4_spmd, body=%wide.region_1.3_spmd.sunk | while | flops 14721026 | bytes 223114064 | solution.py:139
  152.6 10.9 pad.890
  238.4 10.9 pad.889
  256.2 10.9 pad.890
  359.8 10.9 pad.890
  445.7 10.9 pad.889
  463.4 10.9 pad.890
  500.4 32.3 %all-gather.2 = f32[8,16,1536]{2,1,0:T(8,128)S(1)} all-gather(f32[1,16,1536]{2,1,0:T(8,128)} %get-tuple-element.564), channel_id=4, replica_groups=mesh['seq'=8,'batch'=4] {'seq'}, dimensions={0}, use_global_device_ids=true | all-gather | bytes 884736 | tf_op jit(solution)/shard_map/all_gather | solution.py:20
  533.7 11.9 while.97
  545.6 34.0 %all-gather.1 = f32[8,16,1536]{2,1,0:T(8,128)} all-gather(f32[1,16,1536]{2,1,0:T(8,128)} %get-tuple-element.561), channel_id=3, replica_groups=mesh['seq'=8,'batch'=4] {'seq'}, dimensions={0}, use_global_device_ids=true | all-gather | bytes 884736 | tf_op jit(solution)/shard_map/all_gather | solution.py:20
  579.6 11.9 while.95
  591.6 12.4 while.94
  607.0 883.2 %while.98 = (s32[]{:T(128)}, f32[1,16,1536]{2,1,0:T(8,128)S(1)}, f32[16,1536]{1,0:T(8,128)}, f32[4,32,1,3104]{3,1,2,0:T(8,128)}, f32[4,32,1,3104]{3,2,1,0:T(1,12...) while((s32[]{:T(128)}, f32[1,16,1536]{2,1,0:T(8,128)S(1)}, ...), condition=%wide.region_23.24_spmd.clone, body=%wide.region_17.23_spmd.clone.sunk | while | flops 36273152 | bytes 493608896 | solution.py:201
  693.1 10.9 pad.946
  778.4 10.9 pad.961
  796.2 11.1 pad.962
  896.0 10.9 pad.945
  913.8 10.9 pad.946
  999.1 10.9 pad.961
  1016.9 11.1 pad.962
  1134.4 10.9 pad.946
  1219.7 10.9 pad.961
  1237.5 11.1 pad.962
  1337.3 10.9 pad.945
  1355.1 10.9 pad.946
  1440.4 10.9 pad.961
  1458.2 11.1 pad.962
  1526.4 11.3 fusion.44
  1544.0 12.2 fusion.69
  1556.2 43.1 %all-reduce.63 = (f32[768]{0:T(1024)}, f32[4,1536]{1,0:T(4,128)}, f32[1536]{0:T(1024)}, f32[1536]{0:T(1024)}, f32[1536]{0:T(1024)}) all-reduce(f32[768]{0:T(1024)S(1)} %get-tuple-element.805, f32[4,1536]{1,0:T(4,128)S(1)} %pad_maximum_fusion.31, ...), channel_id=1, replica_groups=mesh['seq'=8,'batch'=4] {'seq','batch'}, use_global_device_ids=true, to_apply=%region_26.27 | all-reduce | flops 11520 | bytes 92160 | tf_op jit(solution)/shard_map/psum | solution.py:237
  1600.3 480.7 %all-reduce.67.cloned.1.call-done = (f32[768,3072]{1,0:T(8,128)}, f32[1536,80]{0,1:T(8,128)}, f32[48,1536]{1,0:T(8,128)}, f32[1536,16]{0,1:T(8,128)}, f32[1536,768]{1,0:T(8,128)}) async-done(((f32[768,3072]{1,0:T(8,128)}, f32[1536,80]{0,1:T(8,128)}, f32[48,1536]{1,0:T(8,128)}, f32[1536,16]{0,1:T(8,128)}, f32[1536,768]{1,0:T(8,128)}), (f32[768,3072]{1,0:T(8,128)}, f32[1536,80]{0,1:T(8,128)}, ...) | async-done | bytes 15040528 | tf_op jit(solution)/shard_map/psum | solution.py:237
  (1609 shorter events, 1225.7 us)
Async XLA Ops:
  7.2 26.5 %copy-start = (f32[1536,80]{0,1:T(8,128)S(1)}, f32[1536,80]{0,1:T(8,128)}, u32[]{:S(2)}) copy-start(f32[1536,80]{0,1:T(8,128)} %param.40) | copy-start | bytes 1474564
  7.2 2073.8 %all-reduce.67.cloned.1.call-start = ((), (), s32[]{:S(2)}) async-start(), calls=%async_computation | async-start | bytes 30081024 | tf_op jit(solution)/shard_map/psum | solution.py:237
  16.8 16.9 copy-start.60
  16.9 6.5 collective-permute-start
  22.1 11.6 copy-start.114
  22.1 11.6 copy-start.116
  22.1 11.6 copy-start.118
  22.1 11.6 copy-start.120
  23.4 10.3 copy-start.122
  23.4 11.3 copy-start.132
  33.7 38.0 %copy-start.63 = (f32[128,1536]{1,0:T(8,128)}, f32[128,1536]{1,0:T(8,128)S(1)}, u32[]{:S(2)}) copy-start(f32[128,1536]{1,0:T(8,128)S(1)} %get-tuple-element.907) | copy-start | bytes 2359300
  152.6 10.9 copy-start.29
  256.2 10.9 copy-start.29
  359.8 10.9 copy-start.29
  463.4 10.9 copy-start.29
  500.4 33.3 %copy-start.69 = (f32[1,16,1536]{2,1,0:T(8,128)S(1)}, f32[1,16,1536]{2,1,0:T(8,128)}, u32[]{:S(2)}) copy-start(f32[1,16,1536]{2,1,0:T(8,128)} %custom-call.2) | copy-start | bytes 294916
  533.7 46.0 %copy-start.87 = (f32[1,16,1536]{2,1,0:T(8,128)S(1)}, f32[1,16,1536]{2,1,0:T(8,128)}, u32[]{:S(2)}) copy-start(f32[1,16,1536]{2,1,0:T(8,128)} %custom-call) | copy-start | bytes 294916
  693.1 10.9 copy-start.31
  796.2 11.1 copy-start.30
  913.8 10.9 copy-start.31
  1016.9 11.1 copy-start.30
  1134.4 10.9 copy-start.31
  1237.5 11.1 copy-start.30
  1355.1 10.9 copy-start.31
  1458.2 11.1 copy-start.30
  1513.6 11.1 collective-permute-start.1
  1544.0 12.3 copy-start.129
  1544.0 55.4 %copy-start.102 = (f32[1,128,768]{2,1,0:T(8,128)S(1)}, f32[1,128,768]{2,1,0:T(8,128)}, u32[]{:S(2)}) copy-start(f32[1,128,768]{2,1,0:T(8,128)} %param.47) | copy-start | bytes 1179652
  1544.0 55.4 %copy-start.130 = (f32[128]{0:T(128)S(1)}, f32[128]{0:T(128)}, u32[]{:S(2)}) copy-start(f32[128]{0:T(128)} %get-tuple-element.1005) | copy-start | bytes 1540
  2081.0 10.9 slice-start.1
  2081.0 9.5 copy-start.108
  2081.0 10.9 slice-start.2
  (356 other events, 1008.3 us)
Sparse Core Ops, SparseCore 0:
  1537.8 543.1 all-reduce.66
where the time goes:
time: 2130 us; the launch traced here: 2100 us
  local copies, waits for them, and re-layouts  1010 us (47%)
  waiting for transfers between devices  482 us (23%)
  other arithmetic  379 us (18%)
  blocking collectives  143 us (7%)
  matrix products  65.5 us (3%)
    pad x192, local copies, waits for them, and re-layouts, block_states(): lax.associative_scan(pair_combine, (factor, source), axis=0)  811 us
    psum x1, waiting for transfers between devices, shards(): lax.psum((gain_grad, in_grad, tap_grads, conv_bias_grad, x_proj_grad, ste...  481 us
    add x96, other arithmetic, pair_combine(): return (first[0] * second[0], first[1] * second[0] + second[1])  105 us
    all_gather x3, blocking collectives, prefix(): pieces = jax.tree.map(lambda part: lax.all_gather(part, axis), value)  99.6 us
    add x96, other arithmetic, block_states(): lax.associative_scan(pair_combine, (factor, source), axis=0)  87.8 us
    dot_general x12, matrix products, matmul(): jnp.dot(left, right, precision=MATMUL_ACCURACY, preferred_element_type=jn...  65.5 us
    slice x84, local copies, waits for them, and re-layouts, block_states(): lax.associative_scan(pair_combine, (factor, source), axis=0)  54.1 us
    while x668, local copies, waits for them, and re-layouts  49 us
  transfers between devices with their start and end apart: 3, of which 2 were waited for; matrix products, arithmetic and copies ran while one was open for 1% of the time, Pallas kernels for 0%

commit v1 on v0

--- a/solution.py
+++ b/solution.py
@@ -3,6 +3,7 @@
 import jax.numpy as jnp
 from jax import lax
 from jax.sharding import PartitionSpec as P
+from jax.lax import psum
 
 QB = 32
 MATMUL_ACCURACY = lax.Precision.HIGHEST
@@ -234,20 +235,23 @@
         + flat_cot
     )
     input_grad = input_grad.reshape(seqs, group, width)
-    summed_all = lax.psum(
-        (
-            gain_grad,
-            in_grad,
-            tap_grads,
-            conv_bias_grad,
-            x_proj_grad,
-            step_proj_grad,
-            bias_grad,
-            decay_grad,
-            skip_grad,
-            out_grad,
+    summed_all = psum(
+        psum(
+            (
+                gain_grad,
+                in_grad,
+                tap_grads,
+                conv_bias_grad,
+                x_proj_grad,
+                step_proj_grad,
+                bias_grad,
+                decay_grad,
+                skip_grad,
+                out_grad,
+            ),
+            "batch",
         ),
-        ("seq", "batch"),
+        "seq",
     )
     summed = summed_all[:8]
     skip_sum = summed_all[8]

time: 2130 us -> 2320 us (1.089)
  waiting for transfers between devices: 482 us -> 665 us
    psum x1 -> x2, waiting for transfers between devices: 481 us -> 663 us  [the longest x1 401 us: shards(): psum(psum((gain_grad, in_grad, tap_grads, conv_bias_grad, x_proj_grad, st...]
    psum x1 -> x2, blocking collectives: 43.1 us -> 53.3 us  [the longest x1 41.8 us: shards(): psum(psum((gain_grad, in_grad, tap_grads, conv_bias_grad, x_proj_grad, st...]
  transfers between devices with their start and end apart: 3 -> 4, of which waited for: 2 -> 3; matrix products, arithmetic and copies ran while one was open for 1% -> 1% of each run, Pallas kernels for 0% -> 0%
where the time goes in v1:
time: 2320 us; the launch traced here: 2290 us
  local copies, waits for them, and re-layouts  1000 us (43%)
  waiting for transfers between devices  665 us (29%)
  other arithmetic  379 us (16%)
  blocking collectives  153 us (7%)
  matrix products  65.3 us (3%)
    pad x192, local copies, waits for them, and re-layouts, block_states(): lax.associative_scan(pair_combine, (factor, source), axis=0)  811 us
    psum x1, waiting for transfers between devices, shards(): psum(psum((gain_grad, in_grad, tap_grads, conv_bias_grad, x_proj_grad, st...  401 us
    psum x1, waiting for transfers between devices, shards(): psum((gain_grad, in_grad, tap_grads, conv_bias_grad, x_proj_grad, step_pr...  263 us
    add x96, other arithmetic, pair_combine(): return (first[0] * second[0], first[1] * second[0] + second[1])  105 us
    all_gather x3, blocking collectives, prefix(): pieces = jax.tree.map(lambda part: lax.all_gather(part, axis), value)  99.6 us
    add x96, other arithmetic, block_states(): lax.associative_scan(pair_combine, (factor, source), axis=0)  87.8 us
    dot_general x12, matrix products, matmul(): jnp.dot(left, right, precision=MATMUL_ACCURACY, preferred_element_type=jn...  65.3 us
    slice x84, local copies, waits for them, and re-layouts, block_states(): lax.associative_scan(pair_combine, (factor, source), axis=0)  54.2 us
  transfers between devices with their start and end apart: 4, of which 3 were waited for; matrix products, arithmetic and copies ran while one was open for 1% of the time, Pallas kernels for 0%

profile of v1, /device:TPU:0, one launch (start us, length us, event | category | flops | bytes accessed | tf_op | source)
XLA Modules:
  0.0 2293.6 jit_solution(2735229972882037936)
XLA Ops:
  37.9 33.2 %all-gather.3 = f32[8,1,1536]{2,1,0:T(1,128)S(1)} all-gather(f32[1,1,1536]{2,1,0:T(1,128)S(1)} %reshape.758), channel_id=2, replica_groups=mesh['seq'=8,'batch'=4] {'seq'}, dimensions={0}, use_global_device_ids=true | all-gather | bytes 55296 | tf_op jit(solution)/shard_map/all_gather | solution.py:21
  75.0 414.5 %while.93 = (s32[]{:T(128)}, f32[1,16,1536]{2,1,0:T(8,128)}, f32[4,32,1,1536]{3,2,1,0:T(1,128)}, f32[4,1,16,1536]{3,2,1,0:T(8,128)}, f32[4,32,1,3104]{3,2,1,0:T(...) while((s32[]{:T(128)}, f32[1,16,1536]{2,1,0:T(8,128)}, f32[4,32,1,1536]{3,2,1,0:T(1,128)}, ...), condition=%wide.region_3.4_spmd, body=%wide.region_1.3_spmd.sunk | while | flops 14721026 | bytes 223114064 | solution.py:140
  134.8 10.9 pad.889
  152.6 10.9 pad.890
  238.4 10.9 pad.889
  256.2 10.9 pad.890
  359.9 10.9 pad.890
  463.5 10.9 pad.890
  500.4 32.3 %all-gather.2 = f32[8,16,1536]{2,1,0:T(8,128)S(1)} all-gather(f32[1,16,1536]{2,1,0:T(8,128)} %get-tuple-element.564), channel_id=4, replica_groups=mesh['seq'=8,'batch'=4] {'seq'}, dimensions={0}, use_global_device_ids=true | all-gather | bytes 884736 | tf_op jit(solution)/shard_map/all_gather | solution.py:21
  533.7 11.9 while.97
  545.6 34.0 %all-gather.1 = f32[8,16,1536]{2,1,0:T(8,128)} all-gather(f32[1,16,1536]{2,1,0:T(8,128)} %get-tuple-element.561), channel_id=3, replica_groups=mesh['seq'=8,'batch'=4] {'seq'}, dimensions={0}, use_global_device_ids=true | all-gather | bytes 884736 | tf_op jit(solution)/shard_map/all_gather | solution.py:21
  579.7 11.9 while.95
  591.6 12.4 while.94
  607.1 883.1 %while.98 = (s32[]{:T(128)}, f32[1,16,1536]{2,1,0:T(8,128)S(1)}, f32[16,1536]{1,0:T(8,128)}, f32[4,32,1,3104]{3,1,2,0:T(8,128)}, f32[4,32,1,3104]{3,2,1,0:T(1,12...) while((s32[]{:T(128)}, f32[1,16,1536]{2,1,0:T(8,128)S(1)}, ...), condition=%wide.region_23.24_spmd.clone, body=%wide.region_17.23_spmd.clone.sunk | while | flops 36273152 | bytes 493608896 | solution.py:202
  693.1 10.9 pad.946
  778.5 10.9 pad.961
  796.2 11.1 pad.962
  913.8 10.9 pad.946
  999.1 10.9 pad.961
  1016.9 11.1 pad.962
  1134.4 10.9 pad.946
  1219.7 10.9 pad.961
  1237.5 11.1 pad.962
  1355.1 10.9 pad.946
  1440.4 10.9 pad.961
  1458.2 11.1 pad.962
  1526.2 11.3 fusion.44
  1537.6 262.6 %all-reduce.72.cloned.1.call-done = (f32[768,3072]{1,0:T(8,128)}, f32[1536,80]{0,1:T(8,128)}, f32[48,1536]{1,0:T(8,128)}, f32[1536,16]{0,1:T(8,128)}, f32[1536,768]{1,0:T(8,128)}) async-done(((f32[768,3072]{1,0:T(8,128)}, f32[1536,80]{0,1:T(8,128)}, f32[48,1536]{1,0:T(8,128)}, f32[1536,16]{0,1:T(8,128)}, f32[1536,768]{1,0:T(8,128)}), (f32[768,3072]{1,0:T(8,128)}, f32[1536,80]{0,1:T(8,128)}, ...) | async-done | bytes 15040528 | tf_op jit(solution)/shard_map/psum | solution.py:239
  1806.5 12.0 fusion.69
  1818.6 11.5 all-reduce.65
  1830.1 41.8 %all-reduce.63 = (f32[768]{0:T(1024)}, f32[4,1536]{1,0:T(4,128)}, f32[1536]{0:T(1024)}, f32[1536]{0:T(1024)}, f32[1536]{0:T(1024)}) all-reduce(f32[768]{0:T(1024)S(1)} %get-tuple-element.901, f32[4,1536]{1,0:T(4,128)S(1)} %get-tuple-element.902, f32[1536]{0:T(1024)S(1)} %get-tuple-element.903, ...), channel_id=1, replica_groups=mesh['seq'=8,'batch'=4] {'seq'}, use_global_device_ids=true, to_apply=%region_27.28 | all-reduce | flops 11520 | bytes 92160 | tf_op jit(solution)/shard_map/psum | solution.py:238
  1872.8 400.6 %all-reduce.70.cloned.1.call-done = (f32[768,3072]{1,0:T(8,128)}, f32[1536,80]{0,1:T(8,128)}, f32[48,1536]{1,0:T(8,128)}, f32[1536,16]{0,1:T(8,128)}, f32[1536,768]{1,0:T(8,128)}) async-done(((f32[768,3072]{1,0:T(8,128)}, f32[1536,80]{0,1:T(8,128)}, f32[48,1536]{1,0:T(8,128)}, f32[1536,16]{0,1:T(8,128)}, f32[1536,768]{1,0:T(8,128)}), (f32[768,3072]{1,0:T(8,128)}, f32[1536,80]{0,1:T(8,128)}, ...) | async-done | bytes 15040528 | tf_op jit(solution)/shard_map/psum | solution.py:238
  (1613 shorter events, 1247.4 us)
Async XLA Ops:
  7.2 26.6 %copy-start = (f32[1536,80]{0,1:T(8,128)S(1)}, f32[1536,80]{0,1:T(8,128)}, u32[]{:S(2)}) copy-start(f32[1536,80]{0,1:T(8,128)} %param.40) | copy-start | bytes 1474564
  7.2 1793.0 %all-reduce.72.cloned.1.call-start = ((), (), s32[]{:S(2)}) async-start(), calls=%async_computation.1 | async-start | bytes 30081024 | tf_op jit(solution)/shard_map/psum | solution.py:239
  16.8 16.9 copy-start.60
  16.9 6.5 collective-permute-start
  22.1 11.6 copy-start.114
  22.1 11.6 copy-start.116
  22.1 11.6 copy-start.118
  22.1 11.6 copy-start.120
  23.4 10.3 copy-start.122
  23.4 11.4 copy-start.132
  33.7 38.0 %copy-start.63 = (f32[128,1536]{1,0:T(8,128)}, f32[128,1536]{1,0:T(8,128)S(1)}, u32[]{:S(2)}) copy-start(f32[128,1536]{1,0:T(8,128)S(1)} %get-tuple-element.917) | copy-start | bytes 2359300
  152.6 10.9 copy-start.29
  256.2 10.9 copy-start.29
  359.9 10.9 copy-start.29
  463.5 10.9 copy-start.29
  500.4 33.3 %copy-start.69 = (f32[1,16,1536]{2,1,0:T(8,128)S(1)}, f32[1,16,1536]{2,1,0:T(8,128)}, u32[]{:S(2)}) copy-start(f32[1,16,1536]{2,1,0:T(8,128)} %custom-call.2) | copy-start | bytes 294916
  533.7 46.0 %copy-start.87 = (f32[1,16,1536]{2,1,0:T(8,128)S(1)}, f32[1,16,1536]{2,1,0:T(8,128)}, u32[]{:S(2)}) copy-start(f32[1,16,1536]{2,1,0:T(8,128)} %custom-call) | copy-start | bytes 294916
  693.1 10.9 copy-start.31
  796.2 11.1 copy-start.30
  913.8 10.9 copy-start.31
  1016.9 11.1 copy-start.30
  1134.4 10.9 copy-start.31
  1237.5 11.1 copy-start.30
  1355.1 10.9 copy-start.31
  1458.2 11.1 copy-start.30
  1513.5 11.1 collective-permute-start.1
  1537.5 735.9 %all-reduce.70.cloned.1.call-start = ((), (), s32[]{:S(2)}) async-start(), calls=%async_computation | async-start | bytes 30081024 | tf_op jit(solution)/shard_map/psum | solution.py:238
  1806.5 12.1 copy-start.129
  1806.5 65.4 %copy-start.102 = (f32[1,128,768]{2,1,0:T(8,128)S(1)}, f32[1,128,768]{2,1,0:T(8,128)}, u32[]{:S(2)}) copy-start(f32[1,128,768]{2,1,0:T(8,128)} %param.47) | copy-start | bytes 1179652
  1806.5 65.4 %copy-start.130 = (f32[128]{0:T(128)S(1)}, f32[128]{0:T(128)}, u32[]{:S(2)}) copy-start(f32[128]{0:T(128)} %get-tuple-element.1015) | copy-start | bytes 1540
  2273.5 10.9 slice-start.1
  2273.5 10.9 slice-start.2
  (357 other events, 1017.8 us)
Sparse Core Ops, SparseCore 0:
  1537.7 262.5 all-reduce.71
  1806.4 467.0 all-reduce.69
